TPU v7x, 32 devices: a whole 2x2x4 slice. The times are simulated.
32 devices in a mesh: dp: 8 (over z, x), tensor: 4 (over y, core).
Axes of the slice: x: 2, y: 2, z: 4, core: 2. Of those that a mesh axis runs over, the one named last changes fastest.
Arguments:
- tokens: bfloat16 [16384, 768], P('dp'), may hold values from -6 to 6
- seq_lens: int32 [16], P('dp'), may hold values from 512 to 1024, as said below
- block_sizes: int32 [16], P('dp'), may hold values from 128 to 512
- w_query: bfloat16 [768, 768], P('dp', 'tensor'), may hold values from -0.3125 to 0.3125
- b_query: bfloat16 [768], P('tensor'), may hold values from -3 to 3
- w_key: bfloat16 [768, 768], P('dp', 'tensor'), may hold values from -0.21875 to 0.21875
- w_value: bfloat16 [768, 768], P('dp', 'tensor'), may hold values from -0.21875 to 0.21875
- b_value: bfloat16 [768], P('tensor'), may hold values from -3 to 3
- w_out: bfloat16 [768, 768], P('tensor', 'dp'), may hold values from -1.25 to 1.25
- b_out: bfloat16 [768], P('dp'), may hold values from -2 to 2
- gain_one: bfloat16 [768], P('dp'), may hold values from 0.25 to 1.75
- shift_one: bfloat16 [768], P('dp'), may hold values from -2 to 2
- w_up: bfloat16 [768, 3072], P('dp', 'tensor'), may hold values from -0.21875 to 0.21875
- b_up: bfloat16 [3072], P('tensor'), may hold values from -3 to 3
- w_down: bfloat16 [3072, 768], P('tensor', 'dp'), may hold values from -0.109375 to 0.109375
- b_down: bfloat16 [768], P('dp'), may hold values from -2 to 2
- gain_two: bfloat16 [768], P('dp'), may hold values from 0.25 to 1.75
- shift_two: bfloat16 [768], P('dp'), may hold values from -2 to 2
- cotangent: bfloat16 [16384, 768], P('dp'), may hold values from -6 to 6
Outputs:
- output: bfloat16 [16384, 768], P('dp')
- input_grad: float32 [16384, 768], P('dp', 'tensor')
- grad_w_query: float32 [768, 768], P('dp', 'tensor')
- grad_b_query: float32 [768], P('tensor')
- grad_w_key: float32 [768, 768], P('dp', 'tensor')
- grad_w_value: float32 [768, 768], P('dp', 'tensor')
- grad_b_value: float32 [768], P('tensor')
- grad_w_out: float32 [768, 768], P('tensor', 'dp')
- grad_b_out: float32 [768], P('dp')
- grad_gain_one: float32 [768], P('dp')
- grad_shift_one: float32 [768], P('dp')
- grad_w_up: float32 [768, 3072], P('dp', 'tensor')
- grad_b_up: float32 [3072], P('tensor')
- grad_w_down: float32 [3072, 768], P('tensor', 'dp')
- grad_b_down: float32 [768], P('dp')
- grad_gain_two: float32 [768], P('dp')
- grad_shift_two: float32 [768], P('dp')
Inputs may be any that keep to these rules, and one draw needn't show every extreme that they name: seq_lens[s] counts the key positions of sequence s that any query may see; at least one sequence is whole.
All inputs are finite; a program needn't handle non-finite values.
Results may differ from a plain program's by a relative error of at most 0.015.
The roundings to bfloat16 on the way count: a program that leaves them out, or rounds other values in their place, can miss the bound.
Values may be sent and summed in bfloat16 or wider, within the bound.
A program may use at most 192 MiB of HBM per device.

v0:
```python
import jax
import jax.numpy as jnp
from jax import lax
from jax.sharding import PartitionSpec as P

HEAD = 64
norm_epsilon = 1e-12
inv_root_two = 0.7071067811865476
inv_root_tau = 0.3989422804014327
masked_score = -1000000000.0


def matmul(first_operand, second_operand):
    return jnp.dot(first_operand, second_operand, preferred_element_type=jnp.float32)


def contract_rows(first_operand, second_operand):
    return lax.dot_general(
        first_operand, second_operand, (((0,), (0,)), ((), ())), preferred_element_type=jnp.float32
    )


def contract_cols(first_operand, second_operand):
    return lax.dot_general(
        first_operand, second_operand, (((1,), (1,)), ((), ())), preferred_element_type=jnp.float32
    )


def norm_forward(row_values, gain_row, offset_row):
    row_mean = jnp.mean(row_values, axis=-1, keepdims=True)
    centred = row_values - row_mean
    variance = jnp.mean(centred * centred, axis=-1, keepdims=True)
    inv_scale = lax.rsqrt(variance + norm_epsilon)
    normal_rows = centred * inv_scale
    return (normal_rows * gain_row + offset_row, normal_rows, inv_scale)


def norm_backward(upstream, normal_rows, inv_scale, gain_row):
    scaled = upstream * gain_row
    row_grad = inv_scale * (
        scaled
        - jnp.mean(scaled, axis=-1, keepdims=True)
        - normal_rows * jnp.mean(scaled * normal_rows, axis=-1, keepdims=True)
    )
    return (row_grad, jnp.sum(upstream * normal_rows, axis=0), jnp.sum(upstream, axis=0))


def allowed_mask(first_row, row_total, key_total, seq_length, block_size):
    row_pos = first_row + lax.broadcasted_iota(jnp.int32, (row_total, key_total), 0)
    key_pos = lax.broadcasted_iota(jnp.int32, (row_total, key_total), 1)
    return (key_pos // block_size <= row_pos // block_size) & (key_pos < seq_length)


def attend(query_rows, key_rows, value_rows, seq_length, block_size):
    row_total, local_heads, head_size = query_rows.shape
    block_rows = min(512, row_total)
    block_count = row_total // block_rows
    query_blocks = query_rows.reshape(block_count, block_rows, local_heads, head_size)

    def one_block(block_pair):
        block_index, query_block = block_pair
        scores = jnp.einsum(
            "qhd,khd->hqk", query_block, key_rows, preferred_element_type=jnp.float32
        )
        allowed = allowed_mask(
            block_index * block_rows, block_rows, row_total, seq_length, block_size
        )
        scores = jnp.where(allowed[None], scores, masked_score)
        top_score = jnp.max(scores, axis=-1, keepdims=True)
        exp_scores = jnp.exp(scores - top_score)
        exp_total = jnp.sum(exp_scores, axis=-1, keepdims=True)
        probabilities = (exp_scores / exp_total).astype(jnp.bfloat16)
        context = jnp.einsum(
            "hqk,khd->qhd", probabilities, value_rows, preferred_element_type=jnp.float32
        )
        return (context.astype(jnp.bfloat16), top_score[..., 0] + jnp.log(exp_total[..., 0]))

    contexts, log_sums = lax.map(
        one_block, (jnp.arange(block_count, dtype=jnp.int32), query_blocks)
    )
    return (contexts.reshape(row_total, local_heads * head_size), log_sums)


def attend_back(query_rows, key_rows, value_rows, context_grad, log_sums, seq_length, block_size):
    row_total, local_heads, head_size = query_rows.shape
    block_rows = min(512, row_total)
    block_count = row_total // block_rows
    query_blocks = query_rows.reshape(block_count, block_rows, local_heads, head_size)
    grad_blocks = context_grad.reshape(block_count, block_rows, local_heads, head_size)

    def one_block(running, block_pack):
        key_grad, value_grad = running
        block_index, query_block, grad_block, log_block = block_pack
        scores = jnp.einsum(
            "qhd,khd->hqk", query_block, key_rows, preferred_element_type=jnp.float32
        )
        allowed = allowed_mask(
            block_index * block_rows, block_rows, row_total, seq_length, block_size
        )
        probabilities = jnp.where(allowed[None], jnp.exp(scores - log_block[..., None]), 0.0)
        prob_grad = jnp.einsum(
            "qhd,khd->hqk", grad_block, value_rows, preferred_element_type=jnp.float32
        )
        row_dot = jnp.sum(prob_grad * probabilities, axis=-1, keepdims=True)
        score_grad = (probabilities * (prob_grad - row_dot)).astype(jnp.bfloat16)
        query_grad = jnp.einsum(
            "hqk,khd->qhd", score_grad, key_rows, preferred_element_type=jnp.float32
        )
        key_grad = key_grad + jnp.einsum(
            "hqk,qhd->khd", score_grad, query_block, preferred_element_type=jnp.float32
        )
        value_grad = value_grad + jnp.einsum(
            "hqk,qhd->khd",
            probabilities.astype(jnp.bfloat16),
            grad_block,
            preferred_element_type=jnp.float32,
        )
        return ((key_grad, value_grad), query_grad)

    empty = jnp.zeros((row_total, local_heads, head_size), jnp.float32)
    (key_grad, value_grad), query_grads = lax.scan(
        one_block,
        (empty, empty),
        (jnp.arange(block_count, dtype=jnp.int32), query_blocks, grad_blocks, log_sums),
    )
    width = local_heads * head_size
    return (
        query_grads.reshape(row_total, width),
        key_grad.reshape(row_total, width),
        value_grad.reshape(row_total, width),
    )


def on_device(
    tokens,
    seq_lens,
    block_sizes,
    w_query,
    b_query,
    w_key,
    w_value,
    b_value,
    w_out,
    b_out,
    gain_one,
    shift_one,
    w_up,
    b_up,
    w_down,
    b_down,
    gain_two,
    shift_two,
    cotangent,
):
    micro_total = seq_lens.shape[0]
    seq_rows = tokens.shape[0] // micro_total
    head_cols = w_query.shape[1]
    local_heads = head_cols // HEAD
    model_width = tokens.shape[1]
    own_cols = model_width // lax.axis_size("tensor")
    column_start = lax.axis_index("tensor") * own_cols
    query_bias = b_query.astype(jnp.float32)
    value_bias = b_value.astype(jnp.float32)
    up_bias = b_up.astype(jnp.float32)
    owned = (
        w_query,
        w_key,
        w_value,
        w_out,
        w_up,
        w_down,
        b_out,
        gain_one,
        shift_one,
        b_down,
        gain_two,
        shift_two,
    )

    def shaped(flat_rows):
        return flat_rows.reshape(seq_rows, local_heads, HEAD)

    layer_outputs = []
    input_grads = []
    totals = None
    for micro_index in range(micro_total):
        rows_in = tokens[micro_index * seq_rows : (micro_index + 1) * seq_rows]
        upstream = cotangent[micro_index * seq_rows : (micro_index + 1) * seq_rows].astype(
            jnp.float32
        )
        seq_length = seq_lens[micro_index]
        block_size = block_sizes[micro_index]
        forward_set = (
            lax.all_gather(owned[0], "dp", axis=0, tiled=True),
            lax.all_gather(owned[1], "dp", axis=0, tiled=True),
            lax.all_gather(owned[2], "dp", axis=0, tiled=True),
            lax.all_gather(owned[3], "dp", axis=1, tiled=True),
            lax.all_gather(owned[4], "dp", axis=0, tiled=True),
            lax.all_gather(owned[5], "dp", axis=1, tiled=True),
            lax.all_gather(owned[6], "dp", axis=0, tiled=True),
            lax.all_gather(owned[7], "dp", axis=0, tiled=True),
            lax.all_gather(owned[8], "dp", axis=0, tiled=True),
            lax.all_gather(owned[9], "dp", axis=0, tiled=True),
            lax.all_gather(owned[10], "dp", axis=0, tiled=True),
            lax.all_gather(owned[11], "dp", axis=0, tiled=True),
        )
        (
            full_query,
            full_key,
            full_value,
            full_out,
            full_up,
            full_down,
            full_out_bias,
            full_gain_one,
            full_shift_one,
            full_down_bias,
            full_gain_two,
            full_shift_two,
        ) = forward_set
        out_bias = full_out_bias.astype(jnp.float32)
        down_bias = full_down_bias.astype(jnp.float32)
        first_gain = full_gain_one.astype(jnp.float32)
        first_shift = full_shift_one.astype(jnp.float32)
        second_gain = full_gain_two.astype(jnp.float32)
        second_shift = full_shift_two.astype(jnp.float32)
        query_rows = ((matmul(rows_in, full_query) + query_bias) * 0.125).astype(jnp.bfloat16)
        key_rows = matmul(rows_in, full_key).astype(jnp.bfloat16)
        value_rows = (matmul(rows_in, full_value) + value_bias).astype(jnp.bfloat16)
        context, log_sums = attend(
            shaped(query_rows), shaped(key_rows), shaped(value_rows), seq_length, block_size
        )
        attended = lax.psum(matmul(context, full_out), "tensor") + out_bias
        first_norm, first_hat, first_scale = norm_forward(
            rows_in.astype(jnp.float32) + attended, first_gain, first_shift
        )
        normed = first_norm.astype(jnp.bfloat16)
        expanded = matmul(normed, full_up) + up_bias
        normal_cdf = 0.5 * (1.0 + lax.erf(expanded * inv_root_two))
        hidden = (expanded * normal_cdf).astype(jnp.bfloat16)
        lowered = lax.psum(matmul(hidden, full_down), "tensor") + down_bias
        second_norm, second_hat, second_scale = norm_forward(
            normed.astype(jnp.float32) + lowered, second_gain, second_shift
        )
        layer_outputs.append(second_norm.astype(jnp.bfloat16))
        second_grad, grad_gain_two, grad_shift_two = norm_backward(
            upstream, second_hat, second_scale, second_gain
        )
        down_bias_grad = jnp.sum(second_grad, axis=0)
        second_low = second_grad.astype(jnp.bfloat16)
        down_grad = contract_rows(hidden, second_low)
        hidden_grad = contract_cols(second_low, full_down)
        expanded_grad = hidden_grad * (
            normal_cdf + expanded * jnp.exp(-0.5 * expanded * expanded) * inv_root_tau
        )
        up_bias_grad = jnp.sum(expanded_grad, axis=0)
        expanded_low = expanded_grad.astype(jnp.bfloat16)
        up_grad = contract_rows(normed, expanded_low)
        normed_grad = lax.psum(contract_cols(expanded_low, full_up), "tensor") + second_grad
        first_grad, grad_gain_one, grad_shift_one = norm_backward(
            normed_grad, first_hat, first_scale, first_gain
        )
        out_bias_grad = jnp.sum(first_grad, axis=0)
        first_low = first_grad.astype(jnp.bfloat16)
        out_grad = contract_rows(context, first_low)
        context_grad = contract_cols(first_low, full_out).astype(jnp.bfloat16)
        query_grad, key_grad, value_grad = attend_back(
            shaped(query_rows),
            shaped(key_rows),
            shaped(value_rows),
            shaped(context_grad),
            log_sums,
            seq_length,
            block_size,
        )
        query_grad = query_grad * 0.125
        query_bias_grad = jnp.sum(query_grad, axis=0)
        value_bias_grad = jnp.sum(value_grad, axis=0)
        query_low = query_grad.astype(jnp.bfloat16)
        key_low = key_grad.astype(jnp.bfloat16)
        value_low = value_grad.astype(jnp.bfloat16)
        query_w_grad = contract_rows(rows_in, query_low)
        key_w_grad = contract_rows(rows_in, key_low)
        value_w_grad = contract_rows(rows_in, value_low)
        input_term = (
            contract_cols(query_low, full_query)
            + contract_cols(key_low, full_key)
            + contract_cols(value_low, full_value)
        )
        own_grad = lax.psum_scatter(
            input_term.astype(jnp.bfloat16), "tensor", scatter_dimension=1, tiled=True
        ).astype(jnp.float32)
        input_grads.append(
            own_grad + lax.dynamic_slice_in_dim(first_grad, column_start, own_cols, 1)
        )
        terms = (
            query_w_grad,
            query_bias_grad,
            key_w_grad,
            value_w_grad,
            value_bias_grad,
            out_grad,
            out_bias_grad,
            grad_gain_one,
            grad_shift_one,
            up_grad,
            up_bias_grad,
            down_grad,
            down_bias_grad,
            grad_gain_two,
            grad_shift_two,
        )
        if totals is None:
            totals = terms
        else:
            totals = tuple((running + addend for running, addend in zip(totals, terms)))
    summed = (
        lax.psum_scatter(totals[0], "dp", scatter_dimension=0, tiled=True),
        lax.psum_scatter(totals[2], "dp", scatter_dimension=0, tiled=True),
        lax.psum_scatter(totals[3], "dp", scatter_dimension=0, tiled=True),
        lax.psum_scatter(totals[5], "dp", scatter_dimension=1, tiled=True),
        lax.psum_scatter(totals[9], "dp", scatter_dimension=0, tiled=True),
        lax.psum_scatter(totals[11], "dp", scatter_dimension=1, tiled=True),
        lax.psum_scatter(totals[6], "dp", scatter_dimension=0, tiled=True),
        lax.psum_scatter(totals[7], "dp", scatter_dimension=0, tiled=True),
        lax.psum_scatter(totals[8], "dp", scatter_dimension=0, tiled=True),
        lax.psum_scatter(totals[12], "dp", scatter_dimension=0, tiled=True),
        lax.psum_scatter(totals[13], "dp", scatter_dimension=0, tiled=True),
        lax.psum_scatter(totals[14], "dp", scatter_dimension=0, tiled=True),
    )
    bias_sums = lax.psum((totals[1], totals[4], totals[10]), "dp")
    return (
        jnp.concatenate(layer_outputs, 0),
        jnp.concatenate(input_grads, 0),
        summed[0],
        bias_sums[0],
        summed[1],
        summed[2],
        bias_sums[1],
        summed[3],
        summed[6],
        summed[7],
        summed[8],
        summed[4],
        bias_sums[2],
        summed[5],
        summed[9],
        summed[10],
        summed[11],
    )


def solution(mesh):
    in_specs = (
        P("dp", None),
        P("dp"),
        P("dp"),
        P("dp", "tensor"),
        P("tensor"),
        P("dp", "tensor"),
        P("dp", "tensor"),
        P("tensor"),
        P("tensor", "dp"),
        P("dp"),
        P("dp"),
        P("dp"),
        P("dp", "tensor"),
        P("tensor"),
        P("tensor", "dp"),
        P("dp"),
        P("dp"),
        P("dp"),
        P("dp", None),
    )
    out_specs = (
        P("dp", None),
        P("dp", "tensor"),
        P("dp", "tensor"),
        P("tensor"),
        P("dp", "tensor"),
        P("dp", "tensor"),
        P("tensor"),
        P("tensor", "dp"),
        P("dp"),
        P("dp"),
        P("dp"),
        P("dp", "tensor"),
        P("tensor"),
        P("tensor", "dp"),
        P("dp"),
        P("dp"),
        P("dp"),
    )
    return jax.shard_map(
        on_device, mesh=mesh, in_specs=in_specs, out_specs=out_specs, check_vma=False
    )
```

profile of v0, /device:TPU:0, one launch (start us, length us, event | category | flops | bytes accessed | tf_op | source)
XLA Modules:
  0.0 1132.8 jit_solution(600460367562046693)
XLA Ops:
  8.1 33.1 %all_gather.48 = bf16[768,192]{1,0:T(8,128)(2,1)S(1)} all-gather(bf16[96,192]{1,0:T(8,128)(2,1)} %param.30), channel_id=1, replica_groups=mesh['dp'=8,'tensor'=4] {'dp'}, dimensions={0}, use_global_device_ids=true | all-gather | bytes 331776 | tf_op jit(solution)/shard_map/all_gather | solution.py:194
  46.2 31.1 %all_gather.50 = bf16[768,192]{1,0:T(8,128)(2,1)S(1)} all-gather(bf16[96,192]{1,0:T(8,128)(2,1)S(1)} %copy-done.68), channel_id=1, replica_groups=mesh['dp'=8,'tensor'=4] {'dp'}, dimensions={0}, use_global_device_ids=true | all-gather | bytes 331776 | tf_op jit(solution)/shard_map/all_gather | solution.py:196
  79.4 31.1 %all_gather.49 = bf16[768,192]{1,0:T(8,128)(2,1)S(1)} all-gather(bf16[96,192]{1,0:T(8,128)(2,1)S(1)} %copy-done.69), channel_id=1, replica_groups=mesh['dp'=8,'tensor'=4] {'dp'}, dimensions={0}, use_global_device_ids=true | all-gather | bytes 331776 | tf_op jit(solution)/shard_map/all_gather | solution.py:195
  114.2 21.0 %while.66 = (s32[]{:T(128)}, bf16[2,512,3,64]{1,3,2,0:T(8,128)(2,1)S(1)}, f32[2,3,512]{2,1,0:T(4,128)S(1)}, s32[]{:T(128)}, s32[]{:T(128)}, /*index=5*/s32[2]{0:...) while((s32[]{:T(128)}, ...), condition=%wide.region_3.4_spmd, body=%wide.region_0.3_spmd.sunk | while | flops 419015680 | bytes 22240444 | solution.py:78
  135.8 31.2 %all_gather.51 = bf16[192,768]{0,1:T(8,128)(2,1)S(1)} all-gather(bf16[192,96]{0,1:T(8,128)(2,1)S(1)} %copy.74), channel_id=1, replica_groups=mesh['dp'=8,'tensor'=4] {'dp'}, dimensions={1}, use_global_device_ids=true | all-gather | bytes 331776 | tf_op jit(solution)/shard_map/all_gather | solution.py:197
  168.0 21.0 %while.67 = (s32[]{:T(128)}, bf16[2,512,3,64]{1,3,2,0:T(8,128)(2,1)S(1)}, f32[2,3,512]{2,1,0:T(4,128)S(1)}, s32[]{:T(128)}, s32[]{:T(128)}, /*index=5*/s32[2]{0:...) while((s32[]{:T(128)}, ...), condition=%wide.region_13.14_spmd, body=%wide.region_10.13_spmd.sunk | while | flops 419015680 | bytes 22240444 | solution.py:78
  198.3 38.0 %all-reduce.16 = (bf16[768]{0:T(1024)(128)(2,1)S(1)}, bf16[768]{0:T(1024)(128)(2,1)S(1)}, bf16[768]{0:T(1024)(128)(2,1)S(1)}, bf16[768]{0:T(1024)(128)(2,1)S(1)}...) all-reduce(bf16[768]{0:T(1024)(128)(2,1)S(1)} %dynamic-update-slice, ...), channel_id=1, replica_groups=mesh['dp'=8,'tensor'=4] {'dp'}, use_global_device_ids=true, to_apply=%add | all-reduce | flops 4608 | bytes 18432
  236.4 78.9 %all-reduce.25.cloned.1.call-done = (f32[1024,768]{1,0:T(8,128)}, f32[1024,768]{1,0:T(8,128)}) async-done(((f32[1024,768]{1,0:T(8,128)}, f32[1024,768]{1,0:T(8,128)}), (f32[1024,768]{1,0:T(8,128)}, f32[1024,768]{1,0:T(8,128)})) %all-reduce.25.cloned.1.call-update) | async-done | bytes 6291472 | tf_op jit(solution)/shard_map/psum | solution.py:233
  315.4 4.7 fusion.169
  333.5 4.9 fusion.179
  342.1 119.6 %all-reduce.23.cloned.1.call-done = (f32[1024,768]{1,0:T(8,128)}, f32[1024,768]{1,0:T(8,128)}) async-done(((f32[1024,768]{1,0:T(8,128)}, f32[1024,768]{1,0:T(8,128)}), (f32[1024,768]{1,0:T(8,128)}, f32[1024,768]{1,0:T(8,128)})) %all-reduce.23.cloned.1.call-update) | async-done | bytes 6291472 | tf_op jit(solution)/shard_map/psum | solution.py:241
  461.7 4.2 fusion.167
  471.5 4.6 fusion.161
  489.7 119.9 %all-reduce.21.cloned.1.call-done = (f32[1024,768]{1,0:T(8,128)}, f32[1024,768]{1,0:T(8,128)}) async-done(((f32[1024,768]{1,0:T(8,128)}, f32[1024,768]{1,0:T(8,128)}), (f32[1024,768]{1,0:T(8,128)}, f32[1024,768]{1,0:T(8,128)})) %all-reduce.21.cloned.1.call-update) | async-done | bytes 6291472 | tf_op jit(solution)/shard_map/psum | solution.py:259
  609.6 5.4 multiply_reduce_fusion.3
  628.8 44.0 %while.68 = (s32[]{:T(128)}, f32[1024,3,64]{0,2,1:T(8,128)}, f32[1024,3,64]{0,2,1:T(8,128)}, f32[2,512,3,64]{1,3,2,0:T(8,128)}, bf16[2,512,3,64]{1,3,2,0:T(8,128...) while((s32[]{:T(128)}, f32[1024,3,64]{0,2,1:T(8,128)}, ...), condition=%wide.region_27.28_spmd.clone, body=%wide.region_25.27_spmd.clone.sunk | while | flops 1028402176 | bytes 118828048 | solution.py:121
  675.1 40.6 %while.69 = (s32[]{:T(128)}, f32[1024,3,64]{0,2,1:T(8,128)}, f32[1024,3,64]{0,2,1:T(8,128)}, f32[2,512,3,64]{1,3,2,0:T(8,128)}, bf16[2,512,3,64]{1,3,2,0:T(8,128...) while((s32[]{:T(128)}, f32[1024,3,64]{0,2,1:T(8,128)}, ...), condition=%wide.region_36.37_spmd.clone, body=%wide.region_34.36_spmd.clone.sunk | while | flops 1028402176 | bytes 114159056 | solution.py:121
  743.9 4.0 fusion.143
  761.0 37.7 %all-reduce.12 = (f32[192]{0:T(256)}, f32[192]{0:T(256)}, f32[768]{0:T(1024)S(1)}, f32[768]{0:T(1024)S(1)}, f32[768]{0:T(1024)S(1)}, /*index=5*/f32[768]{0:T(102...) all-reduce(f32[192]{0:T(256)S(1)} %add.515, ...), channel_id=1, replica_groups=mesh['dp'=8,'tensor'=4] {'dp'}, use_global_device_ids=true, to_apply=%region_41.42 | all-reduce | flops 5760 | bytes 46080 | tf_op jit(solution)/shard_map/psum | solution.py:331
  811.7 38.2 %reduce-scatter.33.cloned.1.call-done = f32[96,192]{1,0:T(8,128)} async-done(((f32[768,192]{1,0:T(8,128)}), f32[96,192]{1,0:T(8,128)}) %reduce-scatter.33.cloned.1.call-update) | async-done | bytes 73744
  850.0 65.4 %reduce-scatter.31.cloned.1.call-done = f32[96,192]{1,0:T(8,128)} async-done(((f32[768,192]{1,0:T(8,128)}), f32[96,192]{1,0:T(8,128)}) %reduce-scatter.31.cloned.1.call-update) | async-done | bytes 73744
  915.4 65.7 %reduce-scatter.29.cloned.1.call-done = f32[96,192]{1,0:T(8,128)} async-done(((f32[768,192]{1,0:T(8,128)}), f32[96,192]{1,0:T(8,128)}) %reduce-scatter.29.cloned.1.call-update) | async-done | bytes 73744
  981.1 72.0 %reduce-scatter.23.cloned.1.call-done = f32[768,96]{0,1:T(8,128)} async-done(((f32[768,768]{0,1:T(8,128)}), f32[768,96]{0,1:T(8,128)}) %reduce-scatter.23.cloned.1.call-update) | async-done | bytes 294928 | tf_op jit(solution)/shard_map/reduce_scatter | solution.py:323
  1053.1 72.1 %reduce-scatter.21.cloned.1.call-done = f32[96,768]{1,0:T(8,128)} async-done(((f32[768,768]{1,0:T(8,128)}), f32[96,768]{1,0:T(8,128)}) %reduce-scatter.21.cloned.1.call-update) | async-done | bytes 294928 | tf_op jit(solution)/shard_map/reduce_scatter | solution.py:322
  (521 shorter events, 244.9 us)
Async XLA Ops:
  8.0 36.7 %copy-start.23 = (bf16[2048,768]{1,0:T(8,128)(2,1)S(1)}, bf16[2048,768]{1,0:T(8,128)(2,1)}, u32[]{:S(2)}) copy-start(bf16[2048,768]{1,0:T(8,128)(2,1)} %param.27) | copy-start | bytes 9437188
  8.0 307.3 %all-reduce.25.cloned.1.call-start = ((), (), s32[]{:S(2)}) async-start(), calls=%async_computation.20 | async-start | bytes 12582912 | tf_op jit(solution)/shard_map/psum | solution.py:233
  41.9 35.4 %copy-start.93 = (bf16[192]{0:T(256)(128)(2,1)S(1)}, bf16[192]{0:T(256)(128)(2,1)}, u32[]{:S(2)}) copy-start(bf16[192]{0:T(256)(128)(2,1)} %param.34) | copy-start | bytes 1156
  46.2 33.2 %copy-start.69 = (bf16[96,192]{1,0:T(8,128)(2,1)S(1)}, bf16[96,192]{1,0:T(8,128)(2,1)}, u32[]{:S(2)}) copy-start(bf16[96,192]{1,0:T(8,128)(2,1)} %param.32) | copy-start | bytes 110596
  77.3 34.0 %copy-start.43 = (bf16[768,192]{1,0:T(8,128)(2,1)}, bf16[768,192]{1,0:T(8,128)(2,1)S(1)}, u32[]{:S(2)}) copy-start(bf16[768,192]{1,0:T(8,128)(2,1)S(1)} %all_gather.50) | copy-start | bytes 884740
  77.3 33.2 %copy-start.24 = (bf16[2048,768]{1,0:T(8,128)(2,1)S(1)}, bf16[2048,768]{1,0:T(8,128)(2,1)}, u32[]{:S(2)}) copy-start(bf16[2048,768]{1,0:T(8,128)(2,1)} %param.27) | copy-start | bytes 9437188
  79.4 32.5 %copy-start.64 = (bf16[1024,192]{0,1:T(8,128)(2,1)S(1)}, bf16[1024,192]{0,1:T(8,128)(2,1)}, u32[]{:S(2)}) copy-start(bf16[1024,192]{0,1:T(8,128)(2,1)} %fusion.122) | copy-start | bytes 1179652
  114.2 52.8 %copy-start.63 = (bf16[1024,192]{0,1:T(8,128)(2,1)S(1)}, bf16[1024,192]{0,1:T(8,128)(2,1)}, u32[]{:S(2)}) copy-start(bf16[1024,192]{0,1:T(8,128)(2,1)} %fusion.123) | copy-start | bytes 1179652
  135.7 54.0 %copy-start.57 = (bf16[24,8,2,512]{3,1,2,0:T(8,128)(2,1)}, bf16[24,8,2,512]{3,1,2,0:T(8,128)(2,1)S(1)}, u32[]{:S(2)}) copy-start(bf16[24,8,2,512]{3,1,2,0:T(8,128)(2,1)S(1)} %copy.101) | copy-start | bytes 1179652
  194.4 42.0 %copy-start.85 = (bf16[768]{0:T(1024)(128)(2,1)S(1)}, bf16[768]{0:T(1024)(128)(2,1)}, u32[]{:S(2)}) copy-start(bf16[768]{0:T(1024)(128)(2,1)} %param.40) | copy-start | bytes 4612
  194.4 130.3 %all-gather.3.cloned.1.call-start = ((), (), s32[]{:S(2)}) async-start(), calls=%async_computation.8 | async-start | bytes 1327104 | tf_op jit(solution)/shard_map/all_gather | solution.py:198
  195.0 138.5 %all-gather.5.cloned.1.call-start = ((), (), s32[]{:S(2)}) async-start(), calls=%async_computation.9 | async-start | bytes 1327104 | tf_op jit(solution)/shard_map/all_gather | solution.py:199
  195.6 266.2 %all-reduce.23.cloned.1.call-start = ((), (), s32[]{:S(2)}) async-start(), calls=%async_computation.19 | async-start | bytes 12582912 | tf_op jit(solution)/shard_map/psum | solution.py:241
  324.7 137.1 %copy-start.40 = (bf16[1024,768]{1,0:T(8,128)(2,1)}, bf16[1024,768]{1,0:T(8,128)(2,1)S(1)}, u32[]{:S(2)}) copy-start(bf16[1024,768]{1,0:T(8,128)(2,1)S(1)} %get-tuple-element.1173) | copy-start | bytes 4718596
  341.6 268.0 %all-reduce.21.cloned.1.call-start = ((), (), s32[]{:S(2)}) async-start(), calls=%async_computation.18 | async-start | bytes 12582912 | tf_op jit(solution)/shard_map/psum | solution.py:259
  489.4 312.8 %reduce-scatter.35.cloned.1.call-start = ((), (), s32[]{:S(2)}) async-start(), calls=%async_computation.17 | async-start | bytes 884736
  627.4 176.5 %reduce-scatter.25.cloned.1.call-start = ((), (), s32[]{:S(2)}) async-start(), calls=%async_computation.12 | async-start | bytes 1966080
  628.8 46.3 %copy-start.9 = (bf16[1024,3,64]{0,2,1:T(8,128)(2,1)S(1)}, bf16[1024,3,64]{0,2,1:T(8,128)(2,1)}, u32[]{:S(2)}) copy-start(bf16[1024,3,64]{0,2,1:T(8,128)(2,1)} %copy-done.8) | copy-start | bytes 1179652
  724.0 81.1 %reduce-scatter.27.cloned.1.call-start = ((), (), s32[]{:S(2)}) async-start(), calls=%async_computation.13 | async-start | bytes 1966080
  727.8 122.2 %reduce-scatter.33.cloned.1.call-start = ((), (), s32[]{:S(2)}) async-start(), calls=%async_computation.16 | async-start | bytes 884736
  733.6 181.8 %reduce-scatter.31.cloned.1.call-start = ((), (), s32[]{:S(2)}) async-start(), calls=%async_computation.15 | async-start | bytes 884736
  738.7 242.4 %reduce-scatter.29.cloned.1.call-start = ((), (), s32[]{:S(2)}) async-start(), calls=%async_computation.14 | async-start | bytes 884736
  743.8 309.3 %reduce-scatter.23.cloned.1.call-start = ((), (), s32[]{:S(2)}) async-start(), calls=%async_computation.11 | async-start | bytes 2654208 | tf_op jit(solution)/shard_map/reduce_scatter | solution.py:323
  750.9 374.4 %reduce-scatter.21.cloned.1.call-start = ((), (), s32[]{:S(2)}) async-start(), calls=%async_computation.10 | async-start | bytes 2654208 | tf_op jit(solution)/shard_map/reduce_scatter | solution.py:322
  (115 other events, 433.0 us)
Sparse Core Ops, SparseCore 0:
  194.5 120.7 all-reduce.24
  341.7 119.9 all-reduce.22
  489.6 119.9 all-reduce.20
Sparse Core Ops, SparseCore 1:
  197.1 42.1 all-gather.2
  241.3 40.2 all-gather.4
  627.5 62.7 reduce-scatter.34
  724.1 28.2 reduce-scatter.24
  755.0 28.1 reduce-scatter.26
  787.4 62.6 reduce-scatter.32
  853.7 61.6 reduce-scatter.30
  919.5 61.5 reduce-scatter.28
  985.0 68.0 reduce-scatter.22
  1057.2 68.0 reduce-scatter.20
where the time goes:
time: 1140 us; the launch traced here: 1130 us
  waiting for transfers between devices  633 us (56%)
  blocking collectives  202 us (18%)
  matrix products  137 us (12%)
  other arithmetic  89.8 us (8%)
  local copies, waits for them, and re-layouts  43.1 us (4%)
  between operations  19.9 us (2%)
    unnamed x19, waiting for transfers between devices  171 us
    psum x1, waiting for transfers between devices, on_device(): lax.psum(contract_cols(expanded_low, full_up), 'tensor') + second_grad  120 us
    psum x1, waiting for transfers between devices, on_device(): lowered = lax.psum(matmul(hidden, full_down), 'tensor') + down_bias  120 us
    psum x1, waiting for transfers between devices, on_device(): attended = lax.psum(matmul(context, full_out), 'tensor') + out_bias  78.9 us
    reduce_scatter x1, waiting for transfers between devices, on_device(): lax.psum_scatter(totals[9], 'dp', scatter_dimension=0, tiled=True)  72.1 us
    reduce_scatter x1, waiting for transfers between devices, on_device(): lax.psum_scatter(totals[11], 'dp', scatter_dimension=1, tiled=True)  72 us
    unnamed x1, blocking collectives  38 us
    psum x1, blocking collectives, on_device(): bias_sums = lax.psum((totals[1], totals[4], totals[10]), 'dp')  37.7 us
  transfers between devices with their start and end apart: 13, of which 8 were waited for; matrix products, arithmetic and copies ran while one was open for 14% of the time, Pallas kernels for 0%

commit v1 on v0

--- a/solution.py
+++ b/solution.py
@@ -8,6 +8,13 @@
 inv_root_two = 0.7071067811865476
 inv_root_tau = 0.3989422804014327
 masked_score = -1000000000.0
+
+
+def gather_over(x, name, dim):
+    size = lax.axis_size(name)
+    blocks = jnp.stack([x for _ in range(size)])
+    blocks = lax.all_to_all(blocks, name, split_axis=0, concat_axis=0)
+    return jnp.concatenate(blocks, axis=dim)
 
 
 def matmul(first_operand, second_operand):
@@ -194,7 +201,7 @@
             lax.all_gather(owned[0], "dp", axis=0, tiled=True),
             lax.all_gather(owned[1], "dp", axis=0, tiled=True),
             lax.all_gather(owned[2], "dp", axis=0, tiled=True),
-            lax.all_gather(owned[3], "dp", axis=1, tiled=True),
+            gather_over(owned[3], "dp", 1),
             lax.all_gather(owned[4], "dp", axis=0, tiled=True),
             lax.all_gather(owned[5], "dp", axis=1, tiled=True),
             lax.all_gather(owned[6], "dp", axis=0, tiled=True),

time: 1140 us -> 1120 us (0.982)
  blocking collectives: 202 us -> 170 us
    all_gather x1 -> x0, blocking collectives: 31.2 us -> none  [on_device(): lax.all_gather(owned[3], 'dp', axis=1, tiled=True)]
    unnamed x214 -> x211, local copies, waits for them, and re-layouts: 28.8 us -> 28.7 us
  transfers between devices with their start and end apart: 13 -> 14, of which waited for: 8 -> 8; matrix products, arithmetic and copies ran while one was open for 14% -> 19% of each run, Pallas kernels for 0% -> 0%
where the time goes in v1:
time: 1120 us; the launch traced here: 1110 us
  waiting for transfers between devices  634 us (57%)
  blocking collectives  170 us (15%)
  matrix products  137 us (12%)
  other arithmetic  90 us (8%)
  local copies, waits for them, and re-layouts  46.6 us (4%)
  between operations  19.7 us (2%)
    unnamed x19, waiting for transfers between devices  171 us
    psum x1, waiting for transfers between devices, on_device(): lowered = lax.psum(matmul(hidden, full_down), 'tensor') + down_bias  120 us
    psum x1, waiting for transfers between devices, on_device(): lax.psum(contract_cols(expanded_low, full_up), 'tensor') + second_grad  120 us
    psum x1, waiting for transfers between devices, on_device(): attended = lax.psum(matmul(context, full_out), 'tensor') + out_bias  79.6 us
    reduce_scatter x1, waiting for transfers between devices, on_device(): lax.psum_scatter(totals[9], 'dp', scatter_dimension=0, tiled=True)  72.1 us
    reduce_scatter x1, waiting for transfers between devices, on_device(): lax.psum_scatter(totals[11], 'dp', scatter_dimension=1, tiled=True)  72 us
    psum x1, blocking collectives, on_device(): bias_sums = lax.psum((totals[1], totals[4], totals[10]), 'dp')  37.7 us
    all_gather x1, blocking collectives, on_device(): lax.all_gather(owned[0], 'dp', axis=0, tiled=True)  35.9 us
  transfers between devices with their start and end apart: 14, of which 8 were waited for; matrix products, arithmetic and copies ran while one was open for 19% of the time, Pallas kernels for 0%

profile of v1, /device:TPU:0, one launch (start us, length us, event | category | flops | bytes accessed | tf_op | source)
XLA Modules:
  0.0 1112.3 jit_solution(1171593190797217667)
XLA Ops:
  9.8 7.3 all-to-all-start
  17.1 35.9 %all_gather.44 = bf16[768,192]{1,0:T(8,128)(2,1)S(1)} all-gather(bf16[96,192]{1,0:T(8,128)(2,1)} %param.30), channel_id=1, replica_groups=mesh['dp'=8,'tensor'=4] {'dp'}, dimensions={0}, use_global_device_ids=true | all-gather | bytes 331776 | tf_op jit(solution)/shard_map/all_gather | solution.py:201
  58.0 31.3 %all_gather.46 = bf16[768,192]{1,0:T(8,128)(2,1)S(1)} all-gather(bf16[96,192]{1,0:T(8,128)(2,1)S(1)} %copy-done.68), channel_id=1, replica_groups=mesh['dp'=8,'tensor'=4] {'dp'}, dimensions={0}, use_global_device_ids=true | all-gather | bytes 331776 | tf_op jit(solution)/shard_map/all_gather | solution.py:203
  91.4 31.3 %all_gather.45 = bf16[768,192]{1,0:T(8,128)(2,1)S(1)} all-gather(bf16[96,192]{1,0:T(8,128)(2,1)S(1)} %copy-done.69), channel_id=1, replica_groups=mesh['dp'=8,'tensor'=4] {'dp'}, dimensions={0}, use_global_device_ids=true | all-gather | bytes 331776 | tf_op jit(solution)/shard_map/all_gather | solution.py:202
  126.4 21.5 %while.66 = (s32[]{:T(128)}, bf16[2,512,3,64]{1,3,2,0:T(8,128)(2,1)S(1)}, f32[2,3,512]{2,1,0:T(4,128)S(1)}, s32[]{:T(128)}, s32[]{:T(128)}, /*index=5*/s32[2]{0:...) while((s32[]{:T(128)}, ...), condition=%wide.region_3.4_spmd, body=%wide.region_0.3_spmd.sunk | while | flops 419015680 | bytes 22240444 | solution.py:85
  149.0 21.0 %while.67 = (s32[]{:T(128)}, bf16[2,512,3,64]{1,3,2,0:T(8,128)(2,1)S(1)}, f32[2,3,512]{2,1,0:T(4,128)S(1)}, s32[]{:T(128)}, s32[]{:T(128)}, /*index=5*/s32[2]{0:...) while((s32[]{:T(128)}, ...), condition=%wide.region_13.14_spmd, body=%wide.region_10.13_spmd.sunk | while | flops 419015680 | bytes 22240444 | solution.py:85
  181.5 33.5 %all-reduce.16 = (bf16[768]{0:T(1024)(128)(2,1)S(1)}, bf16[768]{0:T(1024)(128)(2,1)S(1)}, bf16[768]{0:T(1024)(128)(2,1)S(1)}, bf16[768]{0:T(1024)(128)(2,1)S(1)}...) all-reduce(bf16[768]{0:T(1024)(128)(2,1)S(1)} %dynamic-update-slice, ...), channel_id=1, replica_groups=mesh['dp'=8,'tensor'=4] {'dp'}, use_global_device_ids=true, to_apply=%add | all-reduce | flops 4608 | bytes 18432
  215.1 79.6 %all-reduce.25.cloned.1.call-done = (f32[1024,768]{1,0:T(8,128)}, f32[1024,768]{1,0:T(8,128)}) async-done(((f32[1024,768]{1,0:T(8,128)}, f32[1024,768]{1,0:T(8,128)}), (f32[1024,768]{1,0:T(8,128)}, f32[1024,768]{1,0:T(8,128)})) %all-reduce.25.cloned.1.call-update) | async-done | bytes 6291472 | tf_op jit(solution)/shard_map/psum | solution.py:240
  294.6 4.7 fusion.169
  312.8 4.9 fusion.179
  320.9 120.1 %all-reduce.23.cloned.1.call-done = (f32[1024,768]{1,0:T(8,128)}, f32[1024,768]{1,0:T(8,128)}) async-done(((f32[1024,768]{1,0:T(8,128)}, f32[1024,768]{1,0:T(8,128)}), (f32[1024,768]{1,0:T(8,128)}, f32[1024,768]{1,0:T(8,128)})) %all-reduce.23.cloned.1.call-update) | async-done | bytes 6291472 | tf_op jit(solution)/shard_map/psum | solution.py:248
  441.0 4.2 fusion.167
  451.0 4.5 fusion.161
  468.9 120.0 %all-reduce.21.cloned.1.call-done = (f32[1024,768]{1,0:T(8,128)}, f32[1024,768]{1,0:T(8,128)}) async-done(((f32[1024,768]{1,0:T(8,128)}, f32[1024,768]{1,0:T(8,128)}), (f32[1024,768]{1,0:T(8,128)}, f32[1024,768]{1,0:T(8,128)})) %all-reduce.21.cloned.1.call-update) | async-done | bytes 6291472 | tf_op jit(solution)/shard_map/psum | solution.py:266
  589.0 5.4 multiply_reduce_fusion.3
  608.2 44.5 %while.68 = (s32[]{:T(128)}, f32[1024,3,64]{0,2,1:T(8,128)}, f32[1024,3,64]{0,2,1:T(8,128)}, f32[2,512,3,64]{1,3,2,0:T(8,128)}, bf16[2,512,3,64]{1,3,2,0:T(8,128...) while((s32[]{:T(128)}, f32[1024,3,64]{0,2,1:T(8,128)}, ...), condition=%wide.region_27.28_spmd.clone, body=%wide.region_25.27_spmd.clone.sunk | while | flops 1028402176 | bytes 118828048 | solution.py:128
  655.0 40.5 %while.69 = (s32[]{:T(128)}, f32[1024,3,64]{0,2,1:T(8,128)}, f32[1024,3,64]{0,2,1:T(8,128)}, f32[2,512,3,64]{1,3,2,0:T(8,128)}, bf16[2,512,3,64]{1,3,2,0:T(8,128...) while((s32[]{:T(128)}, f32[1024,3,64]{0,2,1:T(8,128)}, ...), condition=%wide.region_36.37_spmd.clone, body=%wide.region_34.36_spmd.clone.sunk | while | flops 1028402176 | bytes 114159056 | solution.py:128
  723.6 4.0 fusion.143
  740.8 37.7 %all-reduce.12 = (f32[192]{0:T(256)}, f32[192]{0:T(256)}, f32[768]{0:T(1024)S(1)}, f32[768]{0:T(1024)S(1)}, f32[768]{0:T(1024)S(1)}, /*index=5*/f32[768]{0:T(102...) all-reduce(f32[192]{0:T(256)S(1)} %add.515, ...), channel_id=1, replica_groups=mesh['dp'=8,'tensor'=4] {'dp'}, use_global_device_ids=true, to_apply=%region_41.42 | all-reduce | flops 5760 | bytes 46080 | tf_op jit(solution)/shard_map/psum | solution.py:338
  791.5 38.3 %reduce-scatter.33.cloned.1.call-done = f32[96,192]{1,0:T(8,128)} async-done(((f32[768,192]{1,0:T(8,128)}), f32[96,192]{1,0:T(8,128)}) %reduce-scatter.33.cloned.1.call-update) | async-done | bytes 73744
  829.8 65.4 %reduce-scatter.31.cloned.1.call-done = f32[96,192]{1,0:T(8,128)} async-done(((f32[768,192]{1,0:T(8,128)}), f32[96,192]{1,0:T(8,128)}) %reduce-scatter.31.cloned.1.call-update) | async-done | bytes 73744
  895.1 65.8 %reduce-scatter.29.cloned.1.call-done = f32[96,192]{1,0:T(8,128)} async-done(((f32[768,192]{1,0:T(8,128)}), f32[96,192]{1,0:T(8,128)}) %reduce-scatter.29.cloned.1.call-update) | async-done | bytes 73744
  960.9 72.0 %reduce-scatter.23.cloned.1.call-done = f32[768,96]{0,1:T(8,128)} async-done(((f32[768,768]{0,1:T(8,128)}), f32[768,96]{0,1:T(8,128)}) %reduce-scatter.23.cloned.1.call-update) | async-done | bytes 294928 | tf_op jit(solution)/shard_map/reduce_scatter | solution.py:330
  1032.9 72.1 %reduce-scatter.21.cloned.1.call-done = f32[96,768]{1,0:T(8,128)} async-done(((f32[768,768]{1,0:T(8,128)}), f32[96,768]{1,0:T(8,128)}) %reduce-scatter.21.cloned.1.call-update) | async-done | bytes 294928 | tf_op jit(solution)/shard_map/reduce_scatter | solution.py:329
  (522 shorter events, 247.8 us)
Async XLA Ops:
  8.0 48.6 %copy-start.23 = (bf16[2048,768]{1,0:T(8,128)(2,1)S(1)}, bf16[2048,768]{1,0:T(8,128)(2,1)}, u32[]{:S(2)}) copy-start(bf16[2048,768]{1,0:T(8,128)(2,1)} %param.27) | copy-start | bytes 9437188
  9.8 161.2 %all-to-all-start = ((bf16[8,192,96]{2,1,0:T(8,128)(2,1)}), bf16[8,192,96]{2,1,0:T(8,128)(2,1)}, u32[]{:S(2)}, u32[]{:S(2)}) async-start(bf16[8,192,96]{2,1,0:T(8,128)(2,1)} %stack.2), calls=%async_computation | async-start | bytes 786432 | tf_op jit(solution)/shard_map/all_to_all | solution.py:16
  17.0 277.6 %all-reduce.25.cloned.1.call-start = ((), (), s32[]{:S(2)}) async-start(), calls=%async_computation.21 | async-start | bytes 12582912 | tf_op jit(solution)/shard_map/psum | solution.py:240
  53.7 35.6 %copy-start.92 = (bf16[192]{0:T(256)(128)(2,1)S(1)}, bf16[192]{0:T(256)(128)(2,1)}, u32[]{:S(2)}) copy-start(bf16[192]{0:T(256)(128)(2,1)} %param.34) | copy-start | bytes 1156
  58.0 33.4 %copy-start.69 = (bf16[96,192]{1,0:T(8,128)(2,1)S(1)}, bf16[96,192]{1,0:T(8,128)(2,1)}, u32[]{:S(2)}) copy-start(bf16[96,192]{1,0:T(8,128)(2,1)} %param.32) | copy-start | bytes 110596
  89.3 34.2 %copy-start.43 = (bf16[768,192]{1,0:T(8,128)(2,1)}, bf16[768,192]{1,0:T(8,128)(2,1)S(1)}, u32[]{:S(2)}) copy-start(bf16[768,192]{1,0:T(8,128)(2,1)S(1)} %all_gather.46) | copy-start | bytes 884740
  89.3 33.5 %copy-start.24 = (bf16[2048,768]{1,0:T(8,128)(2,1)S(1)}, bf16[2048,768]{1,0:T(8,128)(2,1)}, u32[]{:S(2)}) copy-start(bf16[2048,768]{1,0:T(8,128)(2,1)} %param.27) | copy-start | bytes 9437188
  91.4 32.8 %copy-start.64 = (bf16[1024,192]{0,1:T(8,128)(2,1)S(1)}, bf16[1024,192]{0,1:T(8,128)(2,1)}, u32[]{:S(2)}) copy-start(bf16[1024,192]{0,1:T(8,128)(2,1)} %fusion.122) | copy-start | bytes 1179652
  126.4 21.5 %copy-start.63 = (bf16[1024,192]{0,1:T(8,128)(2,1)S(1)}, bf16[1024,192]{0,1:T(8,128)(2,1)}, u32[]{:S(2)}) copy-start(bf16[1024,192]{0,1:T(8,128)(2,1)} %fusion.123) | copy-start | bytes 1179652
  177.4 37.7 %copy-start.84 = (bf16[768]{0:T(1024)(128)(2,1)S(1)}, bf16[768]{0:T(1024)(128)(2,1)}, u32[]{:S(2)}) copy-start(bf16[768]{0:T(1024)(128)(2,1)} %param.40) | copy-start | bytes 4612
  177.4 126.6 %all-gather.3.cloned.1.call-start = ((), (), s32[]{:S(2)}) async-start(), calls=%async_computation.9 | async-start | bytes 1327104 | tf_op jit(solution)/shard_map/all_gather | solution.py:205
  178.0 134.8 %all-gather.5.cloned.1.call-start = ((), (), s32[]{:S(2)}) async-start(), calls=%async_computation.10 | async-start | bytes 1327104 | tf_op jit(solution)/shard_map/all_gather | solution.py:206
  178.6 262.4 %all-reduce.23.cloned.1.call-start = ((), (), s32[]{:S(2)}) async-start(), calls=%async_computation.20 | async-start | bytes 12582912 | tf_op jit(solution)/shard_map/psum | solution.py:248
  304.0 137.0 %copy-start.40 = (bf16[1024,768]{1,0:T(8,128)(2,1)}, bf16[1024,768]{1,0:T(8,128)(2,1)S(1)}, u32[]{:S(2)}) copy-start(bf16[1024,768]{1,0:T(8,128)(2,1)S(1)} %get-tuple-element.1173) | copy-start | bytes 4718596
  320.8 268.1 %all-reduce.21.cloned.1.call-start = ((), (), s32[]{:S(2)}) async-start(), calls=%async_computation.19 | async-start | bytes 12582912 | tf_op jit(solution)/shard_map/psum | solution.py:266
  468.8 313.2 %reduce-scatter.35.cloned.1.call-start = ((), (), s32[]{:S(2)}) async-start(), calls=%async_computation.18 | async-start | bytes 884736
  606.8 176.9 %reduce-scatter.25.cloned.1.call-start = ((), (), s32[]{:S(2)}) async-start(), calls=%async_computation.13 | async-start | bytes 1966080
  608.2 46.8 %copy-start.9 = (bf16[1024,3,64]{0,2,1:T(8,128)(2,1)S(1)}, bf16[1024,3,64]{0,2,1:T(8,128)(2,1)}, u32[]{:S(2)}) copy-start(bf16[1024,3,64]{0,2,1:T(8,128)(2,1)} %copy-done.8) | copy-start | bytes 1179652
  703.8 81.1 %reduce-scatter.27.cloned.1.call-start = ((), (), s32[]{:S(2)}) async-start(), calls=%async_computation.14 | async-start | bytes 1966080
  707.6 122.2 %reduce-scatter.33.cloned.1.call-start = ((), (), s32[]{:S(2)}) async-start(), calls=%async_computation.17 | async-start | bytes 884736
  713.4 181.8 %reduce-scatter.31.cloned.1.call-start = ((), (), s32[]{:S(2)}) async-start(), calls=%async_computation.16 | async-start | bytes 884736
  718.5 242.4 %reduce-scatter.29.cloned.1.call-start = ((), (), s32[]{:S(2)}) async-start(), calls=%async_computation.15 | async-start | bytes 884736
  723.6 309.3 %reduce-scatter.23.cloned.1.call-start = ((), (), s32[]{:S(2)}) async-start(), calls=%async_computation.12 | async-start | bytes 2654208 | tf_op jit(solution)/shard_map/reduce_scatter | solution.py:330
  730.6 374.3 %reduce-scatter.21.cloned.1.call-start = ((), (), s32[]{:S(2)}) async-start(), calls=%async_computation.11 | async-start | bytes 2654208 | tf_op jit(solution)/shard_map/reduce_scatter | solution.py:329
  (115 other events, 422.7 us)
Sparse Core Ops, SparseCore 0:
  177.5 117.0 all-reduce.24
  320.9 119.9 all-reduce.22
  469.0 119.9 all-reduce.20
Sparse Core Ops, SparseCore 1:
  180.1 38.4 all-gather.2
  220.6 40.1 all-gather.4
  606.9 62.7 reduce-scatter.34
  703.9 28.3 reduce-scatter.24
  734.8 28.1 reduce-scatter.26
  767.2 62.5 reduce-scatter.32
  833.5 61.6 reduce-scatter.30
  899.2 61.6 reduce-scatter.28
  964.8 68.0 reduce-scatter.22
  1037.0 67.9 reduce-scatter.20
